TPU v7x, 256 devices: a whole 4x4x8 slice. The times are simulated.
256 devices in a mesh: row: 8 (over y, core), col: 32 (over z, x).
Axes of the slice: x: 4, y: 4, z: 8, core: 2. Of those that a mesh axis runs over, the one named last changes fastest.
Arguments:
- right_side: bfloat16 [8, 32, 256, 512], P(None, 'col'), may hold values from -6 to 6
- inverses: bfloat16 [8, 32, 256, 256], P(None, 'col'), may hold values from -0.375 to 0.375
- factor_blocks: bfloat16 [224, 32, 2, 256, 256], P('row', 'col'), may hold values from -0.03125 to 0.03125
- pattern: int32 [224, 32, 2], P('row', 'col'), may hold values from 0 to 3, as said below
Outputs:
- solution: bfloat16 [8, 32, 256, 512], P(None, 'col')
Inputs may be any that keep to these rules, and one draw needn't show every extreme that they name: The 2 entries of one slot list of pattern name different solved blocks.
All inputs are finite; a program needn't handle non-finite values.
Results may differ from a plain program's by a relative error of at most 0.022.
Values may be sent and summed in bfloat16 or wider, within the bound.
No kernel may reach another device: no remote copies, remote signals or barrier semaphores. Data moves between devices by JAX's collectives and lax.ppermute only.
A program may use at most 128 MiB of HBM per device.

v0:
```python
import jax
import jax.numpy as jnp
from jax import lax
from jax.sharding import PartitionSpec as P

LEVELS = 8


def from_root(value, axis, source):
    kept = jnp.where(lax.axis_index(axis) == source, value, 0).astype(value.dtype)
    return lax.psum(kept, axis)


def contribution(blocks, indices, sources):
    picked = jnp.take(sources, indices, axis=0)
    return jnp.einsum("tkab,tkbn->tan", blocks, picked, preferred_element_type=jnp.float32)


def solve_blocks(inverse_level, totals):
    scaled = totals.astype(jnp.bfloat16)
    return jnp.einsum(
        "tab,tbn->tan", inverse_level, scaled, preferred_element_type=jnp.float32
    ).astype(jnp.bfloat16)


def reduce_solve(partial_value, right_level, inverse_level):
    summed = lax.psum(partial_value.astype(jnp.bfloat16), "row").astype(jnp.float32)
    return solve_blocks(inverse_level, right_level.astype(jnp.float32) - summed)


def spread_sources(solved):
    row_index = lax.axis_index("row")
    row_count = lax.axis_size("row")
    group_count = lax.axis_size("col") // row_count
    pieces = []
    for member in range(group_count):
        pieces.append(from_root(solved, "col", row_index + row_count * member))
    return jnp.concatenate(pieces, axis=0)


def shards(right_side, inverses, factor_blocks, pattern):
    solutions = []
    received = []
    for current in range(LEVELS):
        if current == 0:
            solved = solve_blocks(inverses[0], right_side[0].astype(jnp.float32))
        else:
            partial_value = None
            for earlier in range(current):
                pair_index = current * (current - 1) // 2 + earlier
                term = contribution(
                    factor_blocks[pair_index], pattern[pair_index], received[earlier]
                )
                partial_value = term if partial_value is None else partial_value + term
            solved = reduce_solve(partial_value, right_side[current], inverses[current])
        solutions.append(solved)
        if current + 1 < LEVELS:
            sources = spread_sources(solved)
            received.append(sources)
    return jnp.stack(solutions)


def solution(mesh):
    in_specs = (
        P(None, "col", None, None),
        P(None, "col", None, None),
        P("row", "col", None, None, None),
        P("row", "col", None),
    )
    out_specs = P(None, "col", None, None)
    return jax.shard_map(shards, mesh=mesh, in_specs=in_specs, out_specs=out_specs, check_vma=False)
```

profile of v0, /device:TPU:2, one launch (start us, length us, event | category | flops | bytes accessed | tf_op | source)
XLA Modules:
  0.0 1600.2 jit_solution(14815929831289566410)
XLA Ops:
  6.5 1.9 bitcast_dynamic-update-slice_fusion.6
  10.9 2.5 fusion.303
  13.5 1.9 slice_reduce_fusion.6
  21.0 141.9 %all-reduce.48.cloned.1.call-done = (bf16[1,256,512]{2,1,0:T(8,128)(2,1)}, bf16[1,256,512]{2,1,0:T(8,128)(2,1)}, bf16[1,256,512]{2,1,0:T(8,128)(2,1)}, bf16[1,256,512]{2,1,0:T(8,128)(2,1)}) async-done(((bf16[1,256,512]{2,1,0:T(8,128)(2,1)}, bf16[1,256,512]{2,1,0:T(8,128)(2,1)}, bf16[1,256,512]{2,1,0:T(8,128)(2,1)}, bf16[1,256,512]{2,1,0:T(8,128)(2,1)}), (bf16[1,256,512]{2,1,0:T(8,128)(2,1)}, ...) | async-done | bytes 1048592 | tf_op jit(solution)/shard_map/psum | solution.py:11
  167.4 2.1 fusion.31
  169.6 63.4 %all-reduce.22.cloned.1.call-done = bf16[1,256,512]{1,2,0:T(8,128)(2,1)} async-done(((bf16[1,256,512]{1,2,0:T(8,128)(2,1)}), bf16[1,256,512]{1,2,0:T(8,128)(2,1)}) %all-reduce.22.cloned.1.call-update) | async-done | bytes 262160 | tf_op jit(solution)/shard_map/psum | solution.py:27
  233.1 2.0 bitcast_dynamic-update-slice_fusion.5
  236.7 148.6 %all-reduce.46.cloned.1.call-done = (bf16[1,256,512]{2,1,0:T(8,128)(2,1)}, bf16[1,256,512]{2,1,0:T(8,128)(2,1)}, bf16[1,256,512]{2,1,0:T(8,128)(2,1)}, bf16[1,256,512]{2,1,0:T(8,128)(2,1)}) async-done(((bf16[1,256,512]{2,1,0:T(8,128)(2,1)}, bf16[1,256,512]{2,1,0:T(8,128)(2,1)}, bf16[1,256,512]{2,1,0:T(8,128)(2,1)}, bf16[1,256,512]{2,1,0:T(8,128)(2,1)}), (bf16[1,256,512]{2,1,0:T(8,128)(2,1)}, ...) | async-done | bytes 1048592 | tf_op jit(solution)/shard_map/psum | solution.py:11
  392.1 2.1 fusion.33
  394.4 63.3 %all-reduce.24.cloned.1.call-done = bf16[1,256,512]{1,2,0:T(8,128)(2,1)} async-done(((bf16[1,256,512]{1,2,0:T(8,128)(2,1)}), bf16[1,256,512]{1,2,0:T(8,128)(2,1)}) %all-reduce.24.cloned.1.call-update) | async-done | bytes 262160 | tf_op jit(solution)/shard_map/psum | solution.py:27
  457.7 2.0 bitcast_dynamic-update-slice_fusion.4
  464.4 2.2 convolution_bitcast_fusion.23
  466.6 142.8 %all-reduce.44.cloned.1.call-done = (bf16[1,256,512]{2,1,0:T(8,128)(2,1)}, bf16[1,256,512]{2,1,0:T(8,128)(2,1)}, bf16[1,256,512]{2,1,0:T(8,128)(2,1)}, bf16[1,256,512]{2,1,0:T(8,128)(2,1)}) async-done(((bf16[1,256,512]{2,1,0:T(8,128)(2,1)}, bf16[1,256,512]{2,1,0:T(8,128)(2,1)}, bf16[1,256,512]{2,1,0:T(8,128)(2,1)}, bf16[1,256,512]{2,1,0:T(8,128)(2,1)}), (bf16[1,256,512]{2,1,0:T(8,128)(2,1)}, ...) | async-done | bytes 1048592 | tf_op jit(solution)/shard_map/psum | solution.py:11
  616.2 2.4 fusion.35
  619.4 1.8 copy.84
  621.8 60.3 %all-reduce.26.cloned.1.call-done = bf16[1,256,512]{1,2,0:T(8,128)(2,1)} async-done(((bf16[1,256,512]{1,2,0:T(8,128)(2,1)}), bf16[1,256,512]{1,2,0:T(8,128)(2,1)}) %all-reduce.26.cloned.1.call-update) | async-done | bytes 262160 | tf_op jit(solution)/shard_map/psum | solution.py:27
  682.1 2.0 bitcast_dynamic-update-slice_fusion.3
  689.2 2.3 convolution_bitcast_fusion.20
  692.9 2.3 convolution_bitcast_fusion.19
  695.2 139.2 %all-reduce.42.cloned.1.call-done = (bf16[1,256,512]{2,1,0:T(8,128)(2,1)}, bf16[1,256,512]{2,1,0:T(8,128)(2,1)}, bf16[1,256,512]{2,1,0:T(8,128)(2,1)}, bf16[1,256,512]{2,1,0:T(8,128)(2,1)}) async-done(((bf16[1,256,512]{2,1,0:T(8,128)(2,1)}, bf16[1,256,512]{2,1,0:T(8,128)(2,1)}, bf16[1,256,512]{2,1,0:T(8,128)(2,1)}, bf16[1,256,512]{2,1,0:T(8,128)(2,1)}), (bf16[1,256,512]{2,1,0:T(8,128)(2,1)}, ...) | async-done | bytes 1048592 | tf_op jit(solution)/shard_map/psum | solution.py:11
  837.7 1.7 constant_dynamic-update-slice_fusion.13
  839.4 1.7 constant_dynamic-update-slice_fusion.12
  841.1 2.6 gather_fusion.9
  845.2 2.6 fusion.32
  847.9 1.8 copy.85
  849.7 61.6 %all-reduce.28.cloned.1.call-done = bf16[1,256,512]{1,2,0:T(8,128)(2,1)} async-done(((bf16[1,256,512]{1,2,0:T(8,128)(2,1)}), bf16[1,256,512]{1,2,0:T(8,128)(2,1)}) %all-reduce.28.cloned.1.call-update) | async-done | bytes 262160 | tf_op jit(solution)/shard_map/psum | solution.py:27
  911.3 2.0 bitcast_dynamic-update-slice_fusion.2
  917.3 2.3 convolution_bitcast_fusion.16
  921.0 2.3 convolution_bitcast_fusion.15
  923.3 2.6 gather_fusion.13
  926.0 2.3 convolution_bitcast_fusion.14
  928.3 134.8 %all-reduce.40.cloned.1.call-done = (bf16[1,256,512]{2,1,0:T(8,128)(2,1)}, bf16[1,256,512]{2,1,0:T(8,128)(2,1)}, bf16[1,256,512]{2,1,0:T(8,128)(2,1)}, bf16[1,256,512]{2,1,0:T(8,128)(2,1)}) async-done(((bf16[1,256,512]{2,1,0:T(8,128)(2,1)}, bf16[1,256,512]{2,1,0:T(8,128)(2,1)}, bf16[1,256,512]{2,1,0:T(8,128)(2,1)}, bf16[1,256,512]{2,1,0:T(8,128)(2,1)}), (bf16[1,256,512]{2,1,0:T(8,128)(2,1)}, ...) | async-done | bytes 1048592 | tf_op jit(solution)/shard_map/psum | solution.py:11
  1063.1 1.7 constant_dynamic-update-slice_fusion.19
  1064.8 1.7 constant_dynamic-update-slice_fusion.18
  1066.5 1.7 constant_dynamic-update-slice_fusion.17
  1068.2 1.7 constant_dynamic-update-slice_fusion.16
  1069.8 2.6 gather_fusion.14
  1074.0 2.7 fusion.28
  1076.8 1.8 copy.86
  1078.6 61.6 %all-reduce.30.cloned.1.call-done = bf16[1,256,512]{1,2,0:T(8,128)(2,1)} async-done(((bf16[1,256,512]{1,2,0:T(8,128)(2,1)}), bf16[1,256,512]{1,2,0:T(8,128)(2,1)}) %all-reduce.30.cloned.1.call-update) | async-done | bytes 262160 | tf_op jit(solution)/shard_map/psum | solution.py:27
  1140.2 2.0 bitcast_dynamic-update-slice_fusion.1
  1146.3 2.3 convolution_bitcast_fusion.11
  1150.0 2.3 convolution_bitcast_fusion.10
  1152.4 2.6 gather_fusion.18
  1155.0 2.4 convolution_bitcast_fusion.9
  1157.3 2.6 gather_fusion.19
  1159.9 2.3 convolution_bitcast_fusion.8
  1162.3 130.3 %all-reduce.38.cloned.1.call-done = (bf16[1,256,512]{2,1,0:T(8,128)(2,1)}, bf16[1,256,512]{2,1,0:T(8,128)(2,1)}, bf16[1,256,512]{2,1,0:T(8,128)(2,1)}, bf16[1,256,512]{2,1,0:T(8,128)(2,1)}) async-done(((bf16[1,256,512]{2,1,0:T(8,128)(2,1)}, bf16[1,256,512]{2,1,0:T(8,128)(2,1)}, bf16[1,256,512]{2,1,0:T(8,128)(2,1)}, bf16[1,256,512]{2,1,0:T(8,128)(2,1)}), (bf16[1,256,512]{2,1,0:T(8,128)(2,1)}, ...) | async-done | bytes 1048592 | tf_op jit(solution)/shard_map/psum | solution.py:11
  1292.5 1.7 constant_dynamic-update-slice_fusion.23
  1297.6 1.7 constant_dynamic-update-slice_fusion.20
  1299.2 2.6 gather_fusion.20
  1303.4 2.9 fusion.34
  1306.4 1.8 copy.87
  1308.2 61.5 %all-reduce.32.cloned.1.call-done = bf16[1,256,512]{1,2,0:T(8,128)(2,1)} async-done(((bf16[1,256,512]{1,2,0:T(8,128)(2,1)}), bf16[1,256,512]{1,2,0:T(8,128)(2,1)}) %all-reduce.32.cloned.1.call-update) | async-done | bytes 262160 | tf_op jit(solution)/shard_map/psum | solution.py:27
  1369.8 2.0 bitcast_dynamic-update-slice_fusion
  1378.2 1.8 gather_fusion.24
  1381.4 1.8 gather_fusion.25
  1383.2 2.2 convolution_bitcast_fusion.2
  1385.4 1.8 gather_fusion.26
  1387.2 2.2 convolution_bitcast_fusion.1
  1389.4 132.1 %all-reduce.36.cloned.1.call-done = (bf16[1,256,512]{2,1,0:T(8,128)(2,1)}, bf16[1,256,512]{2,1,0:T(8,128)(2,1)}, bf16[1,256,512]{2,1,0:T(8,128)(2,1)}, bf16[1,256,512]{2,1,0:T(8,128)(2,1)}) async-done(((bf16[1,256,512]{2,1,0:T(8,128)(2,1)}, bf16[1,256,512]{2,1,0:T(8,128)(2,1)}, bf16[1,256,512]{2,1,0:T(8,128)(2,1)}, bf16[1,256,512]{2,1,0:T(8,128)(2,1)}), (bf16[1,256,512]{2,1,0:T(8,128)(2,1)}, ...) | async-done | bytes 1048592 | tf_op jit(solution)/shard_map/psum | solution.py:11
  1525.8 2.4 fusion.36
  1528.4 63.4 %all-reduce.34.cloned.1.call-done = bf16[1,256,512]{1,2,0:T(8,128)(2,1)} async-done(((bf16[1,256,512]{1,2,0:T(8,128)(2,1)}), bf16[1,256,512]{1,2,0:T(8,128)(2,1)}) %all-reduce.34.cloned.1.call-update) | async-done | bytes 262160 | tf_op jit(solution)/shard_map/psum | solution.py:27
  1591.7 2.0 fusion.30
  (159 shorter events, 74.6 us)
Async XLA Ops:
  6.5 156.4 %all-reduce.48.cloned.1.call-start = ((), (), s32[]{:S(2)}) async-start(), calls=%async_computation.13 | async-start | bytes 2097152 | tf_op jit(solution)/shard_map/psum | solution.py:11
  9.5 223.6 %all-reduce.22.cloned.1.call-start = ((), (), s32[]{:S(2)}) async-start(), calls=%async_computation | async-start | bytes 524288 | tf_op jit(solution)/shard_map/psum | solution.py:27
  169.6 215.8 %all-reduce.46.cloned.1.call-start = ((), (), s32[]{:S(2)}) async-start(), calls=%async_computation.12 | async-start | bytes 2097152 | tf_op jit(solution)/shard_map/psum | solution.py:11
  236.0 221.7 %all-reduce.24.cloned.1.call-start = ((), (), s32[]{:S(2)}) async-start(), calls=%async_computation.1 | async-start | bytes 524288 | tf_op jit(solution)/shard_map/psum | solution.py:27
  394.2 215.1 %all-reduce.44.cloned.1.call-start = ((), (), s32[]{:S(2)}) async-start(), calls=%async_computation.11 | async-start | bytes 2097152 | tf_op jit(solution)/shard_map/psum | solution.py:11
  460.7 221.4 %all-reduce.26.cloned.1.call-start = ((), (), s32[]{:S(2)}) async-start(), calls=%async_computation.2 | async-start | bytes 524288 | tf_op jit(solution)/shard_map/psum | solution.py:27
  618.7 215.7 %all-reduce.42.cloned.1.call-start = ((), (), s32[]{:S(2)}) async-start(), calls=%async_computation.10 | async-start | bytes 2097152 | tf_op jit(solution)/shard_map/psum | solution.py:11
  685.2 226.1 %all-reduce.28.cloned.1.call-start = ((), (), s32[]{:S(2)}) async-start(), calls=%async_computation.3 | async-start | bytes 524288 | tf_op jit(solution)/shard_map/psum | solution.py:27
  845.2 80.7 %copy-start.2 = (pred[2]{0:T(512)(128)(4,1)S(1)}, pred[2]{0:T(512)(128)(4,1)}, u32[]{:S(2)}) copy-start(pred[2]{0:T(512)(128)(4,1)} %get-tuple-element.148) | copy-start | bytes 10
  847.8 215.3 %all-reduce.40.cloned.1.call-start = ((), (), s32[]{:S(2)}) async-start(), calls=%async_computation.9 | async-start | bytes 2097152 | tf_op jit(solution)/shard_map/psum | solution.py:11
  913.4 159.1 %copy-start.1 = (pred[2]{0:T(512)(128)(4,1)S(1)}, pred[2]{0:T(512)(128)(4,1)}, u32[]{:S(2)}) copy-start(pred[2]{0:T(512)(128)(4,1)} %get-tuple-element.147) | copy-start | bytes 10
  914.4 159.6 %copy-start.3 = (pred[2]{0:T(512)(128)(4,1)S(1)}, pred[2]{0:T(512)(128)(4,1)}, u32[]{:S(2)}) copy-start(pred[2]{0:T(512)(128)(4,1)} %and_bitcast_fusion.17) | copy-start | bytes 10
  914.4 225.8 %all-reduce.30.cloned.1.call-start = ((), (), s32[]{:S(2)}) async-start(), calls=%async_computation.4 | async-start | bytes 524288 | tf_op jit(solution)/shard_map/psum | solution.py:27
  928.3 218.0 %copy-start.5 = (pred[2]{0:T(512)(128)(4,1)S(1)}, pred[2]{0:T(512)(128)(4,1)}, u32[]{:S(2)}) copy-start(pred[2]{0:T(512)(128)(4,1)} %and_bitcast_fusion.11) | copy-start | bytes 10
  1076.7 215.8 %all-reduce.38.cloned.1.call-start = ((), (), s32[]{:S(2)}) async-start(), calls=%async_computation.8 | async-start | bytes 2097152 | tf_op jit(solution)/shard_map/psum | solution.py:11
  1143.3 226.5 %all-reduce.32.cloned.1.call-start = ((), (), s32[]{:S(2)}) async-start(), calls=%async_computation.5 | async-start | bytes 524288 | tf_op jit(solution)/shard_map/psum | solution.py:27
  1144.9 158.5 %copy-start.4 = (pred[2]{0:T(512)(128)(4,1)S(1)}, pred[2]{0:T(512)(128)(4,1)}, u32[]{:S(2)}) copy-start(pred[2]{0:T(512)(128)(4,1)} %and_bitcast_fusion.12) | copy-start | bytes 10
  1306.3 215.2 %all-reduce.36.cloned.1.call-start = ((), (), s32[]{:S(2)}) async-start(), calls=%async_computation.7 | async-start | bytes 2097152 | tf_op jit(solution)/shard_map/psum | solution.py:11
  1372.9 218.9 %all-reduce.34.cloned.1.call-start = ((), (), s32[]{:S(2)}) async-start(), calls=%async_computation.6 | async-start | bytes 524288 | tf_op jit(solution)/shard_map/psum | solution.py:27
  1376.2 149.5 %copy-start = (bf16[2,256,512]{2,1,0:T(8,128)(2,1)S(1)}, bf16[2,256,512]{2,1,0:T(8,128)(2,1)}, u32[]{:S(2)}) copy-start(bf16[2,256,512]{2,1,0:T(8,128)(2,1)} %gather_fusion.21) | copy-start | bytes 1572868
Sparse Core Ops, SparseCore 0:
  11.2 151.7 all-reduce.47
  169.7 63.3 all-reduce.21
  237.4 147.8 all-reduce.45
  394.3 63.3 all-reduce.23
  461.4 147.8 all-reduce.43
  618.8 63.3 all-reduce.25
  686.5 147.8 all-reduce.41
  848.0 63.3 all-reduce.27
  915.2 147.9 all-reduce.39
  1076.9 63.3 all-reduce.29
  1144.6 147.9 all-reduce.37
  1306.5 63.2 all-reduce.31
  1373.6 147.8 all-reduce.35
  1528.4 63.3 all-reduce.33
where the time goes:
time: 1600 us
  waiting for transfers between devices  1410 us (88%)
  local copies, waits for them, and re-layouts  88.4 us (6%)
  matrix products  74.1 us (5%)
  other arithmetic  18.1 us (1%)
    psum x7, waiting for transfers between devices, from_root(): return lax.psum(kept, axis)  970 us
    psum x7, waiting for transfers between devices, reduce_solve(): lax.psum(partial_value.astype(jnp.bfloat16), 'row').astype(jnp.float32)  435 us
    dot_general x28, matrix products, contribution(): jnp.einsum('tkab,tkbn->tan', blocks, picked, preferred_element_type=jnp.f...  58.2 us
    gather x28, local copies, waits for them, and re-layouts, contribution(): picked = jnp.take(sources, indices, axis=0)  43.3 us
  transfers between devices with their start and end apart: 14, of which 14 were waited for; matrix products, arithmetic and copies ran while one was open for 5% of the time, Pallas kernels for 0%

commit v1 on v0

--- a/solution.py
+++ b/solution.py
@@ -24,7 +24,8 @@
 
 
 def reduce_solve(partial_value, right_level, inverse_level):
-    summed = lax.psum(partial_value.astype(jnp.bfloat16), "row").astype(jnp.float32)
+    create_types = lambda shard_in: jnp.sum(lax.all_gather(shard_in, axis_name="row"), axis=0)
+    summed = create_types(partial_value.astype(jnp.bfloat16)).astype(jnp.float32)
     return solve_blocks(inverse_level, right_level.astype(jnp.float32) - summed)
 
 

time: 1600 us -> 1390 us (0.87)
  waiting for transfers between devices: 1410 us -> 1170 us
    psum x7 -> x0, waiting for transfers between devices: 435 us -> none  [reduce_solve(): lax.psum(partial_value.astype(jnp.bfloat16), 'row').astype(jnp.float32)]
    all_gather x0 -> x7, waiting for transfers between devices: none -> 187 us  [reduce_solve(): lax.all_gather(shard_in, axis_name='row')]
    psum x7, waiting for transfers between devices: 970 us -> 988 us  [from_root(): return lax.psum(kept, axis)]
    unnamed x37 -> x40, local copies, waits for them, and re-layouts: 31.4 us -> 48.2 us
where the time goes in v1:
time: 1390 us
  waiting for transfers between devices  1170 us (84%)
  local copies, waits for them, and re-layouts  103 us (7%)
  matrix products  74.1 us (5%)
  other arithmetic  19.6 us (1%)
  between operations  14.1 us (1%)
    psum x7, waiting for transfers between devices, from_root(): return lax.psum(kept, axis)  988 us
    all_gather x7, waiting for transfers between devices, reduce_solve(): lax.all_gather(shard_in, axis_name='row')  187 us
    dot_general x28, matrix products, contribution(): jnp.einsum('tkab,tkbn->tan', blocks, picked, preferred_element_type=jnp.f...  58.5 us
    unnamed x40, local copies, waits for them, and re-layouts  48.2 us
    gather x28, local copies, waits for them, and re-layouts, contribution(): picked = jnp.take(sources, indices, axis=0)  44.1 us
  transfers between devices with their start and end apart: 14, of which 14 were waited for; matrix products, arithmetic and copies ran while one was open for 5% of the time, Pallas kernels for 0%

profile of v1, /device:TPU:2, one launch (start us, length us, event | category | flops | bytes accessed | tf_op | source)
XLA Modules:
  0.0 1387.1 jit_solution(10423021335103902982)
XLA Ops:
  6.5 2.1 bitcast_dynamic-update-slice_fusion.6
  11.1 151.9 %all-reduce.27.cloned.1.call-done = (bf16[1,256,512]{2,1,0:T(8,128)(2,1)}, bf16[1,256,512]{2,1,0:T(8,128)(2,1)}, bf16[1,256,512]{2,1,0:T(8,128)(2,1)}, bf16[1,256,512]{2,1,0:T(8,128)(2,1)}) async-done(((bf16[1,256,512]{2,1,0:T(8,128)(2,1)}, bf16[1,256,512]{2,1,0:T(8,128)(2,1)}, bf16[1,256,512]{2,1,0:T(8,128)(2,1)}, bf16[1,256,512]{2,1,0:T(8,128)(2,1)}), (bf16[1,256,512]{2,1,0:T(8,128)(2,1)}, ...) | async-done | bytes 1048592 | tf_op jit(solution)/shard_map/psum | solution.py:11
  168.2 2.3 fusion.31
  172.9 26.0 %all-gather.15.cloned.1.call-done = bf16[2048,512]{0,1:T(8,128)(2,1)} async-done(((bf16[256,512]{0,1:T(8,128)(2,1)}), bf16[2048,512]{0,1:T(8,128)(2,1)}) %all-gather.15.cloned.1.call-update) | async-done | bytes 2097168 | tf_op jit(solution)/shard_map/all_gather | solution.py:27
  198.9 2.3 copy.124
  202.7 1.9 bitcast_dynamic-update-slice_fusion.5
  206.3 149.2 %all-reduce.25.cloned.1.call-done = (bf16[1,256,512]{2,1,0:T(8,128)(2,1)}, bf16[1,256,512]{2,1,0:T(8,128)(2,1)}, bf16[1,256,512]{2,1,0:T(8,128)(2,1)}, bf16[1,256,512]{2,1,0:T(8,128)(2,1)}) async-done(((bf16[1,256,512]{2,1,0:T(8,128)(2,1)}, bf16[1,256,512]{2,1,0:T(8,128)(2,1)}, bf16[1,256,512]{2,1,0:T(8,128)(2,1)}, bf16[1,256,512]{2,1,0:T(8,128)(2,1)}), (bf16[1,256,512]{2,1,0:T(8,128)(2,1)}, ...) | async-done | bytes 1048592 | tf_op jit(solution)/shard_map/psum | solution.py:11
  362.3 2.1 fusion.33
  364.6 28.1 %all-gather.17.cloned.1.call-done = bf16[2048,512]{0,1:T(8,128)(2,1)} async-done(((bf16[256,512]{0,1:T(8,128)(2,1)}), bf16[2048,512]{0,1:T(8,128)(2,1)}) %all-gather.17.cloned.1.call-update) | async-done | bytes 2097168 | tf_op jit(solution)/shard_map/all_gather | solution.py:27
  392.7 2.3 copy.125
  396.6 1.9 bitcast_dynamic-update-slice_fusion.4
  401.6 2.2 convolution_bitcast_fusion.23
  403.8 145.7 %all-reduce.23.cloned.1.call-done = (bf16[1,256,512]{2,1,0:T(8,128)(2,1)}, bf16[1,256,512]{2,1,0:T(8,128)(2,1)}, bf16[1,256,512]{2,1,0:T(8,128)(2,1)}, bf16[1,256,512]{2,1,0:T(8,128)(2,1)}) async-done(((bf16[1,256,512]{2,1,0:T(8,128)(2,1)}, bf16[1,256,512]{2,1,0:T(8,128)(2,1)}, bf16[1,256,512]{2,1,0:T(8,128)(2,1)}, bf16[1,256,512]{2,1,0:T(8,128)(2,1)}), (bf16[1,256,512]{2,1,0:T(8,128)(2,1)}, ...) | async-done | bytes 1048592 | tf_op jit(solution)/shard_map/psum | solution.py:11
  556.3 2.4 fusion.35
  559.0 1.8 copy.119
  561.4 25.7 %all-gather.19.cloned.1.call-done = bf16[2048,512]{0,1:T(8,128)(2,1)} async-done(((bf16[256,512]{0,1:T(8,128)(2,1)}), bf16[2048,512]{0,1:T(8,128)(2,1)}) %all-gather.19.cloned.1.call-update) | async-done | bytes 2097168 | tf_op jit(solution)/shard_map/all_gather | solution.py:27
  587.1 2.3 copy.126
  590.9 2.0 bitcast_dynamic-update-slice_fusion.3
  596.8 2.3 convolution_bitcast_fusion.20
  600.5 2.3 convolution_bitcast_fusion.19
  602.8 140.9 %all-reduce.21.cloned.1.call-done = (bf16[1,256,512]{2,1,0:T(8,128)(2,1)}, bf16[1,256,512]{2,1,0:T(8,128)(2,1)}, bf16[1,256,512]{2,1,0:T(8,128)(2,1)}, bf16[1,256,512]{2,1,0:T(8,128)(2,1)}) async-done(((bf16[1,256,512]{2,1,0:T(8,128)(2,1)}, bf16[1,256,512]{2,1,0:T(8,128)(2,1)}, bf16[1,256,512]{2,1,0:T(8,128)(2,1)}, bf16[1,256,512]{2,1,0:T(8,128)(2,1)}), (bf16[1,256,512]{2,1,0:T(8,128)(2,1)}, ...) | async-done | bytes 1048592 | tf_op jit(solution)/shard_map/psum | solution.py:11
  743.8 1.7 constant_dynamic-update-slice_fusion.15
  750.5 2.6 gather_fusion.9
  754.6 2.6 fusion.32
  757.3 1.8 copy.120
  759.1 26.5 %all-gather.21.cloned.1.call-done = bf16[2048,512]{0,1:T(8,128)(2,1)} async-done(((bf16[256,512]{0,1:T(8,128)(2,1)}), bf16[2048,512]{0,1:T(8,128)(2,1)}) %all-gather.21.cloned.1.call-update) | async-done | bytes 2097168 | tf_op jit(solution)/shard_map/all_gather | solution.py:27
  785.6 2.3 copy.127
  789.4 2.0 bitcast_dynamic-update-slice_fusion.2
  795.3 2.3 convolution_bitcast_fusion.16
  799.0 2.3 convolution_bitcast_fusion.15
  801.4 2.6 gather_fusion.13
  804.0 2.4 convolution_bitcast_fusion.14
  806.4 136.0 %all-reduce.19.cloned.1.call-done = (bf16[1,256,512]{2,1,0:T(8,128)(2,1)}, bf16[1,256,512]{2,1,0:T(8,128)(2,1)}, bf16[1,256,512]{2,1,0:T(8,128)(2,1)}, bf16[1,256,512]{2,1,0:T(8,128)(2,1)}) async-done(((bf16[1,256,512]{2,1,0:T(8,128)(2,1)}, bf16[1,256,512]{2,1,0:T(8,128)(2,1)}, bf16[1,256,512]{2,1,0:T(8,128)(2,1)}, bf16[1,256,512]{2,1,0:T(8,128)(2,1)}), (bf16[1,256,512]{2,1,0:T(8,128)(2,1)}, ...) | async-done | bytes 1048592 | tf_op jit(solution)/shard_map/psum | solution.py:11
  942.3 1.7 constant_dynamic-update-slice_fusion.19
  949.0 2.6 gather_fusion.14
  953.2 2.7 fusion.28
  956.2 1.8 copy.121
  958.2 26.0 %all-gather.23.cloned.1.call-done = bf16[2048,512]{0,1:T(8,128)(2,1)} async-done(((bf16[256,512]{0,1:T(8,128)(2,1)}), bf16[2048,512]{0,1:T(8,128)(2,1)}) %all-gather.23.cloned.1.call-update) | async-done | bytes 2097168 | tf_op jit(solution)/shard_map/all_gather | solution.py:27
  984.2 2.3 copy.128
  988.1 2.0 bitcast_dynamic-update-slice_fusion.1
  993.9 2.3 convolution_bitcast_fusion.11
  997.7 2.3 convolution_bitcast_fusion.10
  1000.0 2.6 gather_fusion.18
  1002.6 2.4 convolution_bitcast_fusion.9
  1005.0 2.6 gather_fusion.19
  1007.6 2.3 convolution_bitcast_fusion.8
  1009.9 131.0 %all-reduce.17.cloned.1.call-done = (bf16[1,256,512]{2,1,0:T(8,128)(2,1)}, bf16[1,256,512]{2,1,0:T(8,128)(2,1)}, bf16[1,256,512]{2,1,0:T(8,128)(2,1)}, bf16[1,256,512]{2,1,0:T(8,128)(2,1)}) async-done(((bf16[1,256,512]{2,1,0:T(8,128)(2,1)}, bf16[1,256,512]{2,1,0:T(8,128)(2,1)}, bf16[1,256,512]{2,1,0:T(8,128)(2,1)}, bf16[1,256,512]{2,1,0:T(8,128)(2,1)}), (bf16[1,256,512]{2,1,0:T(8,128)(2,1)}, ...) | async-done | bytes 1048592 | tf_op jit(solution)/shard_map/psum | solution.py:11
  1146.0 1.7 constant_dynamic-update-slice_fusion.20
  1147.6 2.6 gather_fusion.20
  1151.8 2.9 fusion.34
  1154.8 1.8 copy.122
  1156.6 26.4 %all-gather.25.cloned.1.call-done = bf16[2048,512]{0,1:T(8,128)(2,1)} async-done(((bf16[256,512]{0,1:T(8,128)(2,1)}), bf16[2048,512]{0,1:T(8,128)(2,1)}) %all-gather.25.cloned.1.call-update) | async-done | bytes 2097168 | tf_op jit(solution)/shard_map/all_gather | solution.py:27
  1183.1 2.3 copy.129
  1186.9 2.0 bitcast_dynamic-update-slice_fusion
  1195.5 1.8 gather_fusion.24
  1198.7 1.8 gather_fusion.25
  1200.5 2.2 convolution_bitcast_fusion.2
  1202.7 1.8 gather_fusion.26
  1204.5 2.2 convolution_bitcast_fusion.1
  1206.7 133.1 %all-reduce.15.cloned.1.call-done = (bf16[1,256,512]{2,1,0:T(8,128)(2,1)}, bf16[1,256,512]{2,1,0:T(8,128)(2,1)}, bf16[1,256,512]{2,1,0:T(8,128)(2,1)}, bf16[1,256,512]{2,1,0:T(8,128)(2,1)}) async-done(((bf16[1,256,512]{2,1,0:T(8,128)(2,1)}, bf16[1,256,512]{2,1,0:T(8,128)(2,1)}, bf16[1,256,512]{2,1,0:T(8,128)(2,1)}, bf16[1,256,512]{2,1,0:T(8,128)(2,1)}), (bf16[1,256,512]{2,1,0:T(8,128)(2,1)}, ...) | async-done | bytes 1048592 | tf_op jit(solution)/shard_map/psum | solution.py:11
  1344.1 2.5 fusion.36
  1346.7 28.2 %all-gather.27.cloned.1.call-done = bf16[2048,512]{0,1:T(8,128)(2,1)} async-done(((bf16[256,512]{0,1:T(8,128)(2,1)}), bf16[2048,512]{0,1:T(8,128)(2,1)}) %all-gather.27.cloned.1.call-update) | async-done | bytes 2097168 | tf_op jit(solution)/shard_map/all_gather | solution.py:27
  1374.9 2.3 copy.130
  1378.7 1.9 fusion.30
  (169 shorter events, 88.4 us)
Async XLA Ops:
  6.5 164.0 %copy-start = (bf16[8,1,256,512]{3,2,1,0:T(8,128)(2,1)S(1)}, bf16[8,1,256,512]{3,2,1,0:T(8,128)(2,1)}, u32[]{:S(2)}) copy-start(bf16[8,1,256,512]{3,2,1,0:T(8,128)(2,1)} %param.6) | copy-start | bytes 6291460
  6.5 156.5 %all-reduce.27.cloned.1.call-start = ((), (), s32[]{:S(2)}) async-start(), calls=%async_computation.13 | async-start | bytes 2097152 | tf_op jit(solution)/shard_map/psum | solution.py:11
  9.7 189.2 %all-gather.15.cloned.1.call-start = ((), (), s32[]{:S(2)}) async-start(), calls=%async_computation | async-start | bytes 2359296 | tf_op jit(solution)/shard_map/all_gather | solution.py:27
  170.5 185.0 %all-reduce.25.cloned.1.call-start = ((), (), s32[]{:S(2)}) async-start(), calls=%async_computation.12 | async-start | bytes 2097152 | tf_op jit(solution)/shard_map/psum | solution.py:11
  201.1 163.3 %copy-start.2 = (bf16[1,1,256,512]{3,2,1,0:T(8,128)(2,1)S(1)}, bf16[1,1,256,512]{3,2,1,0:T(8,128)(2,1)}, u32[]{:S(2)}) copy-start(bf16[1,1,256,512]{3,2,1,0:T(8,128)(2,1)} %get-tuple-element.67) | copy-start | bytes 786436
  205.6 187.1 %all-gather.17.cloned.1.call-start = ((), (), s32[]{:S(2)}) async-start(), calls=%async_computation.1 | async-start | bytes 2359296 | tf_op jit(solution)/shard_map/all_gather | solution.py:27
  364.4 185.0 %all-reduce.23.cloned.1.call-start = ((), (), s32[]{:S(2)}) async-start(), calls=%async_computation.11 | async-start | bytes 2097152 | tf_op jit(solution)/shard_map/psum | solution.py:11
  396.6 164.2 %copy-start.3 = (s32[28,1,2]{0,2,1:T(2,128)S(1)}, s32[28,1,2]{0,2,1:T(2,128)}, u32[]{:S(2)}) copy-start(s32[28,1,2]{0,2,1:T(2,128)} %param.9) | copy-start | bytes 676
  399.5 187.5 %all-gather.19.cloned.1.call-start = ((), (), s32[]{:S(2)}) async-start(), calls=%async_computation.2 | async-start | bytes 2359296 | tf_op jit(solution)/shard_map/all_gather | solution.py:27
  558.7 185.1 %all-reduce.21.cloned.1.call-start = ((), (), s32[]{:S(2)}) async-start(), calls=%async_computation.10 | async-start | bytes 2097152 | tf_op jit(solution)/shard_map/psum | solution.py:11
  593.9 191.7 %all-gather.21.cloned.1.call-start = ((), (), s32[]{:S(2)}) async-start(), calls=%async_computation.3 | async-start | bytes 2359296 | tf_op jit(solution)/shard_map/all_gather | solution.py:27
  757.3 185.1 %all-reduce.19.cloned.1.call-start = ((), (), s32[]{:S(2)}) async-start(), calls=%async_computation.9 | async-start | bytes 2097152 | tf_op jit(solution)/shard_map/psum | solution.py:11
  792.4 191.8 %all-gather.23.cloned.1.call-start = ((), (), s32[]{:S(2)}) async-start(), calls=%async_computation.4 | async-start | bytes 2359296 | tf_op jit(solution)/shard_map/all_gather | solution.py:27
  955.9 185.0 %all-reduce.17.cloned.1.call-start = ((), (), s32[]{:S(2)}) async-start(), calls=%async_computation.8 | async-start | bytes 2097152 | tf_op jit(solution)/shard_map/psum | solution.py:11
  991.1 192.0 %all-gather.25.cloned.1.call-start = ((), (), s32[]{:S(2)}) async-start(), calls=%async_computation.5 | async-start | bytes 2359296 | tf_op jit(solution)/shard_map/all_gather | solution.py:27
  1154.7 185.1 %all-reduce.15.cloned.1.call-start = ((), (), s32[]{:S(2)}) async-start(), calls=%async_computation.7 | async-start | bytes 2097152 | tf_op jit(solution)/shard_map/psum | solution.py:11
  1189.9 185.0 %all-gather.27.cloned.1.call-start = ((), (), s32[]{:S(2)}) async-start(), calls=%async_computation.6 | async-start | bytes 2359296 | tf_op jit(solution)/shard_map/all_gather | solution.py:27
  1193.5 150.5 %copy-start.1 = (bf16[2,256,512]{2,1,0:T(8,128)(2,1)S(1)}, bf16[2,256,512]{2,1,0:T(8,128)(2,1)}, u32[]{:S(2)}) copy-start(bf16[2,256,512]{2,1,0:T(8,128)(2,1)} %gather_fusion.21) | copy-start | bytes 1572868
Sparse Core Ops, SparseCore 0:
  11.2 151.7 all-reduce.26
  170.6 28.1 all-gather.14
  205.7 149.7 all-reduce.24
  364.5 28.1 all-gather.16
  399.6 149.7 all-reduce.22
  558.8 28.1 all-gather.18
  594.0 149.7 all-reduce.20
  757.4 28.1 all-gather.20
  792.6 149.7 all-reduce.18
  956.0 28.1 all-gather.22
  991.2 149.7 all-reduce.16
  1154.8 28.1 all-gather.24
  1190.0 149.7 all-reduce.14
  1346.7 28.1 all-gather.26
